TPU v7x, 1024 devices: a whole 4x4x32 slice. The times are simulated.
1024 devices in a mesh: row: 64 (over z, core), col: 16 (over y, x).
Axes of the slice: x: 4, y: 4, z: 32, core: 2. Of those that a mesh axis runs over, the one named last changes fastest.
Arguments:
- depth: float32 [4096, 2048], P('row', 'col'), may hold values from 0 to 12, as said below
- elevation: float32 [4096, 2048], P('row', 'col'), may hold values from -4 to 4
- flow_x: float32 [4096, 2048], P('row', 'col'), may hold values from -3 to 3
- flow_y: float32 [4096, 2048], P('row', 'col'), may hold values from -3 to 3
- wet_mask: int32 [4096, 2048], P('row', 'col'), may hold values 0 or 1
- manning_class: int32 [4096, 2048], P('row', 'col'), may hold values from 0 to 7
- manning_table: float32 [8], replicated, may hold values from 0.02 to 0.2
Outputs:
- depth_out: float32 [4096, 2048], P('row', 'col')
- flow_x_out: float32 [4096, 2048], P('row', 'col')
- flow_y_out: float32 [4096, 2048], P('row', 'col')
Inputs may be any that keep to these rules, and one draw needn't show every extreme that they name: `depth`: depth is 0 or positive.
All inputs are finite; a program needn't handle non-finite values. No bound on the sum of `wet_mask` on one device may be relied on, other than what follows from the above.
Results may differ from a plain program's by a relative error of at most 0.000033.
Values sent between devices are 32-bit elements; how exact they have to be, the bound alone decides.
No kernel may reach another device: no remote copies, remote signals or barrier semaphores. Data moves between devices by JAX's collectives and lax.ppermute only.
A program may use at most 32 MiB of HBM per device.

v0:
```python
import jax
import jax.numpy as jnp
from jax import lax
from jax.sharding import PartitionSpec as P

ITERS = 12
CLASSES = 8


GRAVITY = 9.81
SPACING = 30.0
COURANT = 0.7
DRY_FLOOR = 0.01
FLOW_FLOOR = 0.05


def padded_2(x, sides, width):
    for axis, dim in sides:
        peers, length = (lax.axis_size(axis), x.shape[dim])
        up = [(i, (i + 1) % peers) for i in range(peers - 1)]
        down = [(j, i) for i, j in up]
        last = lax.slice_in_dim(x, length - width, length, axis=dim)
        initial = lax.slice_in_dim(x, 0, width, axis=dim)
        before = lax.ppermute(last, axis, up)
        after = lax.ppermute(initial, axis, down)
        x = jnp.concatenate([before, x, after], axis=dim)
    return x


def face_flux(flow_old, surf_low, surf_high, bed_low, bed_high, rough_low, opening, time_step):
    flow_depth = jnp.maximum(surf_low, surf_high) - jnp.maximum(bed_low, bed_high)
    driving = jnp.maximum(flow_depth, 0.0)
    friction_depth = jnp.maximum(flow_depth, FLOW_FLOOR)
    slope = (surf_high - surf_low) / SPACING
    driven = flow_old - GRAVITY * driving * time_step * slope
    damping = 1.0 + GRAVITY * time_step * rough_low * jnp.abs(flow_old) / jnp.exp(
        7.0 / 3.0 * jnp.log(friction_depth)
    )
    return opening * driven / damping


def advance_block(fixed_now, moving, time_step):
    bed = fixed_now[0]
    rough = fixed_now[1]
    opening = fixed_now[2]
    surface = moving[0] + bed
    row_old = moving[1]
    col_old = moving[2]
    rows_new = face_flux(
        row_old[:-1, 1:-1],
        surface[:-1, 1:-1],
        surface[1:, 1:-1],
        bed[:-1, 1:-1],
        bed[1:, 1:-1],
        rough[:-1, 1:-1],
        opening[:-1, 1:-1] * opening[1:, 1:-1],
        time_step,
    )
    cols_new = face_flux(
        col_old[1:-1, :-1],
        surface[1:-1, :-1],
        surface[1:-1, 1:],
        bed[1:-1, :-1],
        bed[1:-1, 1:],
        rough[1:-1, :-1],
        opening[1:-1, :-1] * opening[1:-1, 1:],
        time_step,
    )
    change = rows_new[:-1] - rows_new[1:] + (cols_new[:, :-1] - cols_new[:, 1:])
    depth_next = jnp.maximum(moving[0][1:-1, 1:-1] + time_step / SPACING * change, 0.0)
    return jnp.stack([depth_next, rows_new[1:], cols_new[:, 1:]])


def per_device(depth, elevation, flow_x, flow_y, wet_mask, manning_class, manning_table):
    rough_sq = jnp.zeros(depth.shape, jnp.float32)
    for class_id in range(CLASSES):
        rough_sq = rough_sq + jnp.where(
            manning_class == class_id, manning_table[class_id] * manning_table[class_id], 0.0
        )
    wet_open = wet_mask.astype(jnp.float32)
    fixed_fields = jnp.stack([elevation, rough_sq, wet_open])
    state = jnp.stack([depth, flow_x, flow_y])
    tile_rows = depth.shape[0]
    tile_cols = depth.shape[1]
    reach = 1

    def one_round(counter, state_now):
        padded = padded_2(
            jnp.concatenate([fixed_fields, state_now], axis=0), (("row", 1), ("col", 2)), reach
        )
        fixed_block = padded[:3]
        moving = padded[3:]
        owned = moving[0, reach : reach + tile_rows, reach : reach + tile_cols]
        local_bound = jnp.min(COURANT * SPACING / jnp.sqrt(GRAVITY * jnp.maximum(owned, DRY_FLOOR)))
        time_step = lax.pmin(local_bound, ("row", "col"))
        moving = advance_block(fixed_block, moving, time_step)
        return moving

    final = lax.fori_loop(0, ITERS // reach, one_round, state)
    return (final[0], final[1], final[2])


def solution(mesh):
    in_specs = (
        P("row", "col"),
        P("row", "col"),
        P("row", "col"),
        P("row", "col"),
        P("row", "col"),
        P("row", "col"),
        P(),
    )
    out_specs = (P("row", "col"), P("row", "col"), P("row", "col"))
    return jax.shard_map(
        per_device, mesh=mesh, in_specs=in_specs, out_specs=out_specs, check_vma=False
    )
```

profile of v0, /device:TPU:1, one launch (start us, length us, event | category | flops | bytes accessed | tf_op | source)
XLA Modules:
  0.0 2075.8 jit_solution(13013910807468224601)
XLA Ops:
  0.6 1.6 fusion.20
  13.6 0.7 copy-done
  14.4 2060.8 %while.10 = (s32[]{:T(128)}, f32[3,64,128]{2,1,0:T(8,128)S(1)}, f32[1,64,128]{2,1,0:T(8,128)S(1)}, f32[1,64,128]{2,1,0:T(8,128)S(1)}, f32[1,64,128]{2,1,0:T(8,128)S(1)}, /*index=5*/s32[]{:T(128)}, f32[]{:T(128)}, f32[]{:T(128)}) while((s32[]{:T(128)}, f32[3,64,128]{2,1,0:T(8,128)S(1)}, f32[1,64,128]{2,1,0:T(8,128)S(1)}, ...), condition=%wide.region_3.4_spmd, body=%wide.region_0.3_spmd.sunk | while | flops 761896 | bytes 2869781 | solution.py:99
  14.4 16.0 collective-permute-start
  30.5 1.9 collective-permute-start.1
  32.4 1.1 collective-permute-done.1
  33.7 1.3 collective-permute-start.2
  35.0 4.0 collective-permute-start.3
  39.6 160.0 %pmin.8 = f32[]{:T(128)} all-reduce(f32[]{:T(128)} %multiply_reduce_fusion.2), channel_id=1, replica_groups=mesh['row'=64,'col'=16] {'row','col'}, use_global_device_ids=true, to_apply=%region_2.2 | all-reduce | flops 1 | bytes 8 | tf_op jit(solution)/shard_map/while/body/eval_jaxpr/pmin | solution.py:95
  201.7 2.6 collective-permute-start
  204.3 3.4 collective-permute-start.1
  208.6 1.3 collective-permute-start.2
  209.9 4.0 collective-permute-start.3
  214.5 155.4 %pmin.8 = f32[]{:T(128)} all-reduce(f32[]{:T(128)} %multiply_reduce_fusion.2), channel_id=1, replica_groups=mesh['row'=64,'col'=16] {'row','col'}, use_global_device_ids=true, to_apply=%region_2.2 | all-reduce | flops 1 | bytes 8 | tf_op jit(solution)/shard_map/while/body/eval_jaxpr/pmin | solution.py:95
  372.0 2.6 collective-permute-start
  374.6 3.8 collective-permute-start.1
  379.3 1.3 collective-permute-start.2
  380.6 4.0 collective-permute-start.3
  385.2 155.1 %pmin.8 = f32[]{:T(128)} all-reduce(f32[]{:T(128)} %multiply_reduce_fusion.2), channel_id=1, replica_groups=mesh['row'=64,'col'=16] {'row','col'}, use_global_device_ids=true, to_apply=%region_2.2 | all-reduce | flops 1 | bytes 8 | tf_op jit(solution)/shard_map/while/body/eval_jaxpr/pmin | solution.py:95
  542.4 2.6 collective-permute-start
  545.0 3.3 collective-permute-start.1
  549.2 1.3 collective-permute-start.2
  550.5 4.0 collective-permute-start.3
  555.1 155.3 %pmin.8 = f32[]{:T(128)} all-reduce(f32[]{:T(128)} %multiply_reduce_fusion.2), channel_id=1, replica_groups=mesh['row'=64,'col'=16] {'row','col'}, use_global_device_ids=true, to_apply=%region_2.2 | all-reduce | flops 1 | bytes 8 | tf_op jit(solution)/shard_map/while/body/eval_jaxpr/pmin | solution.py:95
  712.6 2.6 collective-permute-start
  715.2 4.0 collective-permute-start.1
  720.1 1.3 collective-permute-start.2
  721.4 4.0 collective-permute-start.3
  726.0 155.1 %pmin.8 = f32[]{:T(128)} all-reduce(f32[]{:T(128)} %multiply_reduce_fusion.2), channel_id=1, replica_groups=mesh['row'=64,'col'=16] {'row','col'}, use_global_device_ids=true, to_apply=%region_2.2 | all-reduce | flops 1 | bytes 8 | tf_op jit(solution)/shard_map/while/body/eval_jaxpr/pmin | solution.py:95
  883.2 2.6 collective-permute-start
  885.8 3.0 collective-permute-start.1
  889.6 1.3 collective-permute-start.2
  890.9 4.0 collective-permute-start.3
  895.6 155.7 %pmin.8 = f32[]{:T(128)} all-reduce(f32[]{:T(128)} %multiply_reduce_fusion.2), channel_id=1, replica_groups=mesh['row'=64,'col'=16] {'row','col'}, use_global_device_ids=true, to_apply=%region_2.2 | all-reduce | flops 1 | bytes 8 | tf_op jit(solution)/shard_map/while/body/eval_jaxpr/pmin | solution.py:95
  1053.4 2.6 collective-permute-start
  1056.0 4.0 collective-permute-start.1
  1060.8 1.3 collective-permute-start.2
  1062.1 4.0 collective-permute-start.3
  1066.8 154.9 %pmin.8 = f32[]{:T(128)} all-reduce(f32[]{:T(128)} %multiply_reduce_fusion.2), channel_id=1, replica_groups=mesh['row'=64,'col'=16] {'row','col'}, use_global_device_ids=true, to_apply=%region_2.2 | all-reduce | flops 1 | bytes 8 | tf_op jit(solution)/shard_map/while/body/eval_jaxpr/pmin | solution.py:95
  1223.8 2.6 collective-permute-start
  1226.4 3.0 collective-permute-start.1
  1230.3 1.3 collective-permute-start.2
  1231.6 4.0 collective-permute-start.3
  1236.2 155.7 %pmin.8 = f32[]{:T(128)} all-reduce(f32[]{:T(128)} %multiply_reduce_fusion.2), channel_id=1, replica_groups=mesh['row'=64,'col'=16] {'row','col'}, use_global_device_ids=true, to_apply=%region_2.2 | all-reduce | flops 1 | bytes 8 | tf_op jit(solution)/shard_map/while/body/eval_jaxpr/pmin | solution.py:95
  1394.1 2.6 collective-permute-start
  1396.6 3.8 collective-permute-start.1
  1401.3 1.3 collective-permute-start.2
  1402.6 4.0 collective-permute-start.3
  1407.2 155.1 %pmin.8 = f32[]{:T(128)} all-reduce(f32[]{:T(128)} %multiply_reduce_fusion.2), channel_id=1, replica_groups=mesh['row'=64,'col'=16] {'row','col'}, use_global_device_ids=true, to_apply=%region_2.2 | all-reduce | flops 1 | bytes 8 | tf_op jit(solution)/shard_map/while/body/eval_jaxpr/pmin | solution.py:95
  1564.5 2.6 collective-permute-start
  1567.0 3.0 collective-permute-start.1
  1570.9 1.3 collective-permute-start.2
  1572.2 4.0 collective-permute-start.3
  1576.8 155.6 %pmin.8 = f32[]{:T(128)} all-reduce(f32[]{:T(128)} %multiply_reduce_fusion.2), channel_id=1, replica_groups=mesh['row'=64,'col'=16] {'row','col'}, use_global_device_ids=true, to_apply=%region_2.2 | all-reduce | flops 1 | bytes 8 | tf_op jit(solution)/shard_map/while/body/eval_jaxpr/pmin | solution.py:95
  1734.6 2.6 collective-permute-start
  1737.1 4.0 collective-permute-start.1
  1742.0 1.3 collective-permute-start.2
  1743.3 4.0 collective-permute-start.3
  1747.9 154.9 %pmin.8 = f32[]{:T(128)} all-reduce(f32[]{:T(128)} %multiply_reduce_fusion.2), channel_id=1, replica_groups=mesh['row'=64,'col'=16] {'row','col'}, use_global_device_ids=true, to_apply=%region_2.2 | all-reduce | flops 1 | bytes 8 | tf_op jit(solution)/shard_map/while/body/eval_jaxpr/pmin | solution.py:95
  1905.0 2.6 collective-permute-start
  1907.6 3.0 collective-permute-start.1
  1911.4 1.3 collective-permute-start.2
  1912.7 4.0 collective-permute-start.3
  1917.4 155.7 %pmin.8 = f32[]{:T(128)} all-reduce(f32[]{:T(128)} %multiply_reduce_fusion.2), channel_id=1, replica_groups=mesh['row'=64,'col'=16] {'row','col'}, use_global_device_ids=true, to_apply=%region_2.2 | all-reduce | flops 1 | bytes 8 | tf_op jit(solution)/shard_map/while/body/eval_jaxpr/pmin | solution.py:95
  (242 shorter events, 27.9 us)
Async XLA Ops:
  0.6 11.4 copy-start.1
  12.1 0.8 copy-start.2
  12.1 0.8 copy-start.5
  12.8 0.8 copy-start.3
  12.8 0.8 copy-start.4
  13.6 0.8 copy-start
  14.4 18.0 collective-permute-start
  30.5 3.1 collective-permute-start.1
  33.7 167.2 %collective-permute-start.2 = (f32[6,66,1]{2,1,0:T(8,128)S(1)}, f32[6,66,1]{2,1,0:T(8,128)S(1)}, u32[]{:S(2)}, u32[]{:S(2)}) collective-permute-start(f32[6,66,1]{2,1,0:T(8,128)S(1)} %get-tuple-element.111), channel_id=1, source_target_pairs={{1,0},{2,1},{3,2},{4,3},{5,4},{6,5},{7,6},{8,7},{9,8},{10,9},{11,1... | collective-permute-start | bytes 4760 | tf_op jit(solution)/shard_map/while/body/eval_jaxpr/ppermute | solution.py:25
  35.0 165.9 %collective-permute-start.3 = (f32[6,66,1]{2,1,0:T(8,128)S(1)}, f32[6,66,1]{2,1,0:T(8,128)S(1)}, u32[]{:S(2)}, u32[]{:S(2)}) collective-permute-start(f32[6,66,1]{2,1,0:T(8,128)S(1)} %get-tuple-element.112), channel_id=1, source_target_pairs={{0,1},{1,2},{2,3},{3,4},{4,5},{5,6},{6,7},{7,8},{8,9},{9,10},{10,1... | collective-permute-start | bytes 4760 | tf_op jit(solution)/shard_map/while/body/eval_jaxpr/ppermute | solution.py:24
  201.7 6.0 collective-permute-start
  204.3 4.1 collective-permute-start.1
  208.6 162.6 %collective-permute-start.2 = (f32[6,66,1]{2,1,0:T(8,128)S(1)}, f32[6,66,1]{2,1,0:T(8,128)S(1)}, u32[]{:S(2)}, u32[]{:S(2)}) collective-permute-start(f32[6,66,1]{2,1,0:T(8,128)S(1)} %get-tuple-element.111), channel_id=1, source_target_pairs={{1,0},{2,1},{3,2},{4,3},{5,4},{6,5},{7,6},{8,7},{9,8},{10,9},{11,1... | collective-permute-start | bytes 4760 | tf_op jit(solution)/shard_map/while/body/eval_jaxpr/ppermute | solution.py:25
  209.9 161.3 %collective-permute-start.3 = (f32[6,66,1]{2,1,0:T(8,128)S(1)}, f32[6,66,1]{2,1,0:T(8,128)S(1)}, u32[]{:S(2)}, u32[]{:S(2)}) collective-permute-start(f32[6,66,1]{2,1,0:T(8,128)S(1)} %get-tuple-element.112), channel_id=1, source_target_pairs={{0,1},{1,2},{2,3},{3,4},{4,5},{5,6},{6,7},{7,8},{8,9},{9,10},{10,1... | collective-permute-start | bytes 4760 | tf_op jit(solution)/shard_map/while/body/eval_jaxpr/ppermute | solution.py:24
  372.0 6.4 collective-permute-start
  374.6 4.6 collective-permute-start.1
  379.3 162.3 %collective-permute-start.2 = (f32[6,66,1]{2,1,0:T(8,128)S(1)}, f32[6,66,1]{2,1,0:T(8,128)S(1)}, u32[]{:S(2)}, u32[]{:S(2)}) collective-permute-start(f32[6,66,1]{2,1,0:T(8,128)S(1)} %get-tuple-element.111), channel_id=1, source_target_pairs={{1,0},{2,1},{3,2},{4,3},{5,4},{6,5},{7,6},{8,7},{9,8},{10,9},{11,1... | collective-permute-start | bytes 4760 | tf_op jit(solution)/shard_map/while/body/eval_jaxpr/ppermute | solution.py:25
  380.6 161.0 %collective-permute-start.3 = (f32[6,66,1]{2,1,0:T(8,128)S(1)}, f32[6,66,1]{2,1,0:T(8,128)S(1)}, u32[]{:S(2)}, u32[]{:S(2)}) collective-permute-start(f32[6,66,1]{2,1,0:T(8,128)S(1)} %get-tuple-element.112), channel_id=1, source_target_pairs={{0,1},{1,2},{2,3},{3,4},{4,5},{5,6},{6,7},{7,8},{8,9},{9,10},{10,1... | collective-permute-start | bytes 4760 | tf_op jit(solution)/shard_map/while/body/eval_jaxpr/ppermute | solution.py:24
  542.4 5.9 collective-permute-start
  545.0 4.1 collective-permute-start.1
  549.2 162.5 %collective-permute-start.2 = (f32[6,66,1]{2,1,0:T(8,128)S(1)}, f32[6,66,1]{2,1,0:T(8,128)S(1)}, u32[]{:S(2)}, u32[]{:S(2)}) collective-permute-start(f32[6,66,1]{2,1,0:T(8,128)S(1)} %get-tuple-element.111), channel_id=1, source_target_pairs={{1,0},{2,1},{3,2},{4,3},{5,4},{6,5},{7,6},{8,7},{9,8},{10,9},{11,1... | collective-permute-start | bytes 4760 | tf_op jit(solution)/shard_map/while/body/eval_jaxpr/ppermute | solution.py:25
  550.5 161.2 %collective-permute-start.3 = (f32[6,66,1]{2,1,0:T(8,128)S(1)}, f32[6,66,1]{2,1,0:T(8,128)S(1)}, u32[]{:S(2)}, u32[]{:S(2)}) collective-permute-start(f32[6,66,1]{2,1,0:T(8,128)S(1)} %get-tuple-element.112), channel_id=1, source_target_pairs={{0,1},{1,2},{2,3},{3,4},{4,5},{5,6},{6,7},{7,8},{8,9},{9,10},{10,1... | collective-permute-start | bytes 4760 | tf_op jit(solution)/shard_map/while/body/eval_jaxpr/ppermute | solution.py:24
  712.6 6.6 collective-permute-start
  715.2 4.7 collective-permute-start.1
  720.1 162.3 %collective-permute-start.2 = (f32[6,66,1]{2,1,0:T(8,128)S(1)}, f32[6,66,1]{2,1,0:T(8,128)S(1)}, u32[]{:S(2)}, u32[]{:S(2)}) collective-permute-start(f32[6,66,1]{2,1,0:T(8,128)S(1)} %get-tuple-element.111), channel_id=1, source_target_pairs={{1,0},{2,1},{3,2},{4,3},{5,4},{6,5},{7,6},{8,7},{9,8},{10,9},{11,1... | collective-permute-start | bytes 4760 | tf_op jit(solution)/shard_map/while/body/eval_jaxpr/ppermute | solution.py:25
  721.4 161.0 %collective-permute-start.3 = (f32[6,66,1]{2,1,0:T(8,128)S(1)}, f32[6,66,1]{2,1,0:T(8,128)S(1)}, u32[]{:S(2)}, u32[]{:S(2)}) collective-permute-start(f32[6,66,1]{2,1,0:T(8,128)S(1)} %get-tuple-element.112), channel_id=1, source_target_pairs={{0,1},{1,2},{2,3},{3,4},{4,5},{5,6},{6,7},{7,8},{8,9},{9,10},{10,1... | collective-permute-start | bytes 4760 | tf_op jit(solution)/shard_map/while/body/eval_jaxpr/ppermute | solution.py:24
  883.2 5.6 collective-permute-start
  885.8 3.7 collective-permute-start.1
  889.6 162.9 %collective-permute-start.2 = (f32[6,66,1]{2,1,0:T(8,128)S(1)}, f32[6,66,1]{2,1,0:T(8,128)S(1)}, u32[]{:S(2)}, u32[]{:S(2)}) collective-permute-start(f32[6,66,1]{2,1,0:T(8,128)S(1)} %get-tuple-element.111), channel_id=1, source_target_pairs={{1,0},{2,1},{3,2},{4,3},{5,4},{6,5},{7,6},{8,7},{9,8},{10,9},{11,1... | collective-permute-start | bytes 4760 | tf_op jit(solution)/shard_map/while/body/eval_jaxpr/ppermute | solution.py:25
  890.9 161.6 %collective-permute-start.3 = (f32[6,66,1]{2,1,0:T(8,128)S(1)}, f32[6,66,1]{2,1,0:T(8,128)S(1)}, u32[]{:S(2)}, u32[]{:S(2)}) collective-permute-start(f32[6,66,1]{2,1,0:T(8,128)S(1)} %get-tuple-element.112), channel_id=1, source_target_pairs={{0,1},{1,2},{2,3},{3,4},{4,5},{5,6},{6,7},{7,8},{8,9},{9,10},{10,1... | collective-permute-start | bytes 4760 | tf_op jit(solution)/shard_map/while/body/eval_jaxpr/ppermute | solution.py:24
  1053.4 6.6 collective-permute-start
  1056.0 4.7 collective-permute-start.1
  1060.8 162.2 %collective-permute-start.2 = (f32[6,66,1]{2,1,0:T(8,128)S(1)}, f32[6,66,1]{2,1,0:T(8,128)S(1)}, u32[]{:S(2)}, u32[]{:S(2)}) collective-permute-start(f32[6,66,1]{2,1,0:T(8,128)S(1)} %get-tuple-element.111), channel_id=1, source_target_pairs={{1,0},{2,1},{3,2},{4,3},{5,4},{6,5},{7,6},{8,7},{9,8},{10,9},{11,1... | collective-permute-start | bytes 4760 | tf_op jit(solution)/shard_map/while/body/eval_jaxpr/ppermute | solution.py:25
  1062.1 160.9 %collective-permute-start.3 = (f32[6,66,1]{2,1,0:T(8,128)S(1)}, f32[6,66,1]{2,1,0:T(8,128)S(1)}, u32[]{:S(2)}, u32[]{:S(2)}) collective-permute-start(f32[6,66,1]{2,1,0:T(8,128)S(1)} %get-tuple-element.112), channel_id=1, source_target_pairs={{0,1},{1,2},{2,3},{3,4},{4,5},{5,6},{6,7},{7,8},{8,9},{9,10},{10,1... | collective-permute-start | bytes 4760 | tf_op jit(solution)/shard_map/while/body/eval_jaxpr/ppermute | solution.py:24
  1223.8 5.6 collective-permute-start
  1226.4 3.7 collective-permute-start.1
  1230.3 162.9 %collective-permute-start.2 = (f32[6,66,1]{2,1,0:T(8,128)S(1)}, f32[6,66,1]{2,1,0:T(8,128)S(1)}, u32[]{:S(2)}, u32[]{:S(2)}) collective-permute-start(f32[6,66,1]{2,1,0:T(8,128)S(1)} %get-tuple-element.111), channel_id=1, source_target_pairs={{1,0},{2,1},{3,2},{4,3},{5,4},{6,5},{7,6},{8,7},{9,8},{10,9},{11,1... | collective-permute-start | bytes 4760 | tf_op jit(solution)/shard_map/while/body/eval_jaxpr/ppermute | solution.py:25
  1231.6 161.6 %collective-permute-start.3 = (f32[6,66,1]{2,1,0:T(8,128)S(1)}, f32[6,66,1]{2,1,0:T(8,128)S(1)}, u32[]{:S(2)}, u32[]{:S(2)}) collective-permute-start(f32[6,66,1]{2,1,0:T(8,128)S(1)} %get-tuple-element.112), channel_id=1, source_target_pairs={{0,1},{1,2},{2,3},{3,4},{4,5},{5,6},{6,7},{7,8},{8,9},{9,10},{10,1... | collective-permute-start | bytes 4760 | tf_op jit(solution)/shard_map/while/body/eval_jaxpr/ppermute | solution.py:24
  1394.1 6.4 collective-permute-start
  1396.6 4.5 collective-permute-start.1
  1401.3 162.3 %collective-permute-start.2 = (f32[6,66,1]{2,1,0:T(8,128)S(1)}, f32[6,66,1]{2,1,0:T(8,128)S(1)}, u32[]{:S(2)}, u32[]{:S(2)}) collective-permute-start(f32[6,66,1]{2,1,0:T(8,128)S(1)} %get-tuple-element.111), channel_id=1, source_target_pairs={{1,0},{2,1},{3,2},{4,3},{5,4},{6,5},{7,6},{8,7},{9,8},{10,9},{11,1... | collective-permute-start | bytes 4760 | tf_op jit(solution)/shard_map/while/body/eval_jaxpr/ppermute | solution.py:25
  1402.6 161.0 %collective-permute-start.3 = (f32[6,66,1]{2,1,0:T(8,128)S(1)}, f32[6,66,1]{2,1,0:T(8,128)S(1)}, u32[]{:S(2)}, u32[]{:S(2)}) collective-permute-start(f32[6,66,1]{2,1,0:T(8,128)S(1)} %get-tuple-element.112), channel_id=1, source_target_pairs={{0,1},{1,2},{2,3},{3,4},{4,5},{5,6},{6,7},{7,8},{8,9},{9,10},{10,1... | collective-permute-start | bytes 4760 | tf_op jit(solution)/shard_map/while/body/eval_jaxpr/ppermute | solution.py:24
  1564.5 5.6 collective-permute-start
  1567.0 3.7 collective-permute-start.1
  1570.9 162.8 %collective-permute-start.2 = (f32[6,66,1]{2,1,0:T(8,128)S(1)}, f32[6,66,1]{2,1,0:T(8,128)S(1)}, u32[]{:S(2)}, u32[]{:S(2)}) collective-permute-start(f32[6,66,1]{2,1,0:T(8,128)S(1)} %get-tuple-element.111), channel_id=1, source_target_pairs={{1,0},{2,1},{3,2},{4,3},{5,4},{6,5},{7,6},{8,7},{9,8},{10,9},{11,1... | collective-permute-start | bytes 4760 | tf_op jit(solution)/shard_map/while/body/eval_jaxpr/ppermute | solution.py:25
  1572.2 161.5 %collective-permute-start.3 = (f32[6,66,1]{2,1,0:T(8,128)S(1)}, f32[6,66,1]{2,1,0:T(8,128)S(1)}, u32[]{:S(2)}, u32[]{:S(2)}) collective-permute-start(f32[6,66,1]{2,1,0:T(8,128)S(1)} %get-tuple-element.112), channel_id=1, source_target_pairs={{0,1},{1,2},{2,3},{3,4},{4,5},{5,6},{6,7},{7,8},{8,9},{9,10},{10,1... | collective-permute-start | bytes 4760 | tf_op jit(solution)/shard_map/while/body/eval_jaxpr/ppermute | solution.py:24
  1734.6 6.6 collective-permute-start
  1737.1 4.7 collective-permute-start.1
  1742.0 162.1 %collective-permute-start.2 = (f32[6,66,1]{2,1,0:T(8,128)S(1)}, f32[6,66,1]{2,1,0:T(8,128)S(1)}, u32[]{:S(2)}, u32[]{:S(2)}) collective-permute-start(f32[6,66,1]{2,1,0:T(8,128)S(1)} %get-tuple-element.111), channel_id=1, source_target_pairs={{1,0},{2,1},{3,2},{4,3},{5,4},{6,5},{7,6},{8,7},{9,8},{10,9},{11,1... | collective-permute-start | bytes 4760 | tf_op jit(solution)/shard_map/while/body/eval_jaxpr/ppermute | solution.py:25
  1743.3 160.8 %collective-permute-start.3 = (f32[6,66,1]{2,1,0:T(8,128)S(1)}, f32[6,66,1]{2,1,0:T(8,128)S(1)}, u32[]{:S(2)}, u32[]{:S(2)}) collective-permute-start(f32[6,66,1]{2,1,0:T(8,128)S(1)} %get-tuple-element.112), channel_id=1, source_target_pairs={{0,1},{1,2},{2,3},{3,4},{4,5},{5,6},{6,7},{7,8},{8,9},{9,10},{10,1... | collective-permute-start | bytes 4760 | tf_op jit(solution)/shard_map/while/body/eval_jaxpr/ppermute | solution.py:24
  1905.0 5.6 collective-permute-start
  1907.6 3.7 collective-permute-start.1
  1911.4 162.9 %collective-permute-start.2 = (f32[6,66,1]{2,1,0:T(8,128)S(1)}, f32[6,66,1]{2,1,0:T(8,128)S(1)}, u32[]{:S(2)}, u32[]{:S(2)}) collective-permute-start(f32[6,66,1]{2,1,0:T(8,128)S(1)} %get-tuple-element.111), channel_id=1, source_target_pairs={{1,0},{2,1},{3,2},{4,3},{5,4},{6,5},{7,6},{8,7},{9,8},{10,9},{11,1... | collective-permute-start | bytes 4760 | tf_op jit(solution)/shard_map/while/body/eval_jaxpr/ppermute | solution.py:25
  1912.7 161.6 %collective-permute-start.3 = (f32[6,66,1]{2,1,0:T(8,128)S(1)}, f32[6,66,1]{2,1,0:T(8,128)S(1)}, u32[]{:S(2)}, u32[]{:S(2)}) collective-permute-start(f32[6,66,1]{2,1,0:T(8,128)S(1)} %get-tuple-element.112), channel_id=1, source_target_pairs={{0,1},{1,2},{2,3},{3,4},{4,5},{5,6},{6,7},{7,8},{8,9},{9,10},{10,1... | collective-permute-start | bytes 4760 | tf_op jit(solution)/shard_map/while/body/eval_jaxpr/ppermute | solution.py:24
where the time goes:
time: 2080 us
  blocking collectives  1870 us (90%)
  starting transfers between devices  148 us (7%)
    pmin x12, blocking collectives, one_round(): time_step = lax.pmin(local_bound, ('row', 'col'))  1870 us
    ppermute x24, starting transfers between devices, padded_2(): before = lax.ppermute(last, axis, up)  88.2 us
    ppermute x24, starting transfers between devices, padded_2(): after = lax.ppermute(initial, axis, down)  59.8 us
  transfers between devices with their start and end apart: 48, of which 12 were waited for; matrix products, arithmetic and copies ran while one was open for 0% of the time, Pallas kernels for 0%

commit v1 on v0

v1 whole, which is shorter than its diff:
```python
import jax
import jax.numpy as jnp
from jax import lax
from jax.experimental import pallas as pl
from jax.experimental.pallas import tpu as pltpu
from jax.sharding import PartitionSpec as P

ITERS = 12
CLASSES = 8
HALO = ITERS

GRAVITY = 9.81
SPACING = 30.0
COURANT = 0.7
DRY_FLOOR = 0.01
FLOW_FLOOR = 0.05


def neighbours(axis):
    peers = lax.axis_size(axis)
    up = [(i, i + 1) for i in range(peers - 1)]
    down = [(j, i) for i, j in up]
    return up, down


def with_halo(fields):
    rows, cols = fields.shape[1:]
    up, down = neighbours("row")
    before = lax.ppermute(fields[:, rows - HALO :], "row", up)
    after = lax.ppermute(fields[:, :HALO], "row", down)
    fields = jnp.concatenate([fields, after, before], axis=1)
    up, down = neighbours("col")
    before = lax.ppermute(fields[:, :, cols - HALO :], "col", up)
    after = lax.ppermute(fields[:, :, :HALO], "col", down)
    gap = jnp.zeros((*fields.shape[:2], cols - 2 * HALO), fields.dtype)
    return jnp.concatenate([fields, after, gap, before], axis=2)


def next_of(x, axis):
    return pltpu.roll(x, x.shape[axis] - 1, axis)


def previous_of(x, axis):
    return pltpu.roll(x, 1, axis)


def face_flux(flow_old, surface, surf_high, bed_max, rough, opening, time_step):
    flow_depth = jnp.maximum(surface, surf_high) - bed_max
    driving = jnp.maximum(flow_depth, 0.0)
    friction_depth = jnp.maximum(flow_depth, FLOW_FLOOR)
    slope = (surf_high - surface) / SPACING
    driven = flow_old - GRAVITY * driving * time_step * slope
    damping = 1.0 + GRAVITY * time_step * rough * jnp.abs(flow_old) * jnp.exp(
        -7.0 / 3.0 * jnp.log(friction_depth)
    )
    return opening * driven / damping


def step_kernel(tile, gathered, state, fixed, state_out, bound_out):
    deepest = jnp.max(gathered[...], axis=(0, 1), keepdims=True)
    time_step = COURANT * SPACING / jnp.sqrt(GRAVITY * jnp.maximum(deepest, DRY_FLOOR))
    depth = state[0]
    bed = fixed[0]
    rough = fixed[1]
    opening = fixed[2]
    surface = depth + bed
    flows = []
    for axis in (0, 1):
        flows.append(
            face_flux(
                state[1 + axis],
                surface,
                next_of(surface, axis),
                jnp.maximum(bed, next_of(bed, axis)),
                rough,
                opening * next_of(opening, axis),
                time_step,
            )
        )
    rows_new, cols_new = flows
    change = previous_of(rows_new, 0) - rows_new + (previous_of(cols_new, 1) - cols_new)
    depth = jnp.maximum(depth + time_step / SPACING * change, 0.0)
    state_out[0] = depth
    state_out[1] = rows_new
    state_out[2] = cols_new
    rows, cols = tile
    own = jnp.max(depth[:rows, :cols], axis=(0, 1), keepdims=True)
    bound_out[...] = jnp.broadcast_to(own, bound_out.shape)


def per_device(depth, elevation, flow_x, flow_y, wet_mask, manning_class, manning_table):
    rough_sq = jnp.zeros(depth.shape, jnp.float32)
    for class_id in range(CLASSES):
        rough_sq = rough_sq + jnp.where(
            manning_class == class_id, manning_table[class_id] * manning_table[class_id], 0.0
        )
    wet_open = wet_mask.astype(jnp.float32)
    rows, cols = depth.shape
    row_peers, col_peers = lax.axis_size("row"), lax.axis_size("col")
    padded = with_halo(jnp.stack([depth, flow_x, flow_y, elevation, rough_sq, wet_open]))
    state, fixed = padded[:3], padded[3:]

    def everywhere(bound):
        over_col = lax.all_to_all(bound, "col", 0, 0, tiled=True)
        merged = jnp.max(over_col, axis=0, keepdims=True)
        return lax.all_to_all(jnp.broadcast_to(merged, (row_peers, 128)), "row", 0, 0, tiled=True)

    step = pl.pallas_call(
        lambda *refs: step_kernel((rows, cols), *refs),
        out_shape=(
            jax.ShapeDtypeStruct(state.shape, jnp.float32),
            jax.ShapeDtypeStruct((col_peers, 128), jnp.float32),
        ),
        name="flood_step",
    )
    bound = jnp.broadcast_to(jnp.max(depth), (col_peers, 128))

    def one_round(counter, carry):
        state, bound = carry
        return step(everywhere(bound), state, fixed)

    state, bound = lax.fori_loop(0, ITERS, one_round, (state, bound))
    final = state[:, :rows, :cols]
    return (final[0], final[1], final[2])


def solution(mesh):
    in_specs = (
        P("row", "col"),
        P("row", "col"),
        P("row", "col"),
        P("row", "col"),
        P("row", "col"),
        P("row", "col"),
        P(),
    )
    out_specs = (P("row", "col"), P("row", "col"), P("row", "col"))
    return jax.shard_map(
        per_device, mesh=mesh, in_specs=in_specs, out_specs=out_specs, check_vma=False
    )
```

time: 2080 us -> 566 us (0.27)
  blocking collectives: 1870 us -> 111 us
  waiting for transfers between devices: 9.05 us -> 266 us
  local copies, waits for them, and re-layouts: 6.64 us -> 30.4 us
  starting transfers between devices: 148 us -> 127 us
    pmin x12 -> x0, blocking collectives: 1870 us -> none  [one_round(): time_step = lax.pmin(local_bound, ('row', 'col'))]
    all_to_all x0 -> x12, waiting for transfers between devices: none -> 260 us  [everywhere(): lax.all_to_all(jnp.broadcast_to(merged, (row_peers, 128)), 'row', 0, 0, t...]
    ppermute x48 -> x4, starting transfers between devices: 148 us -> 23.2 us  [the longest x1 16 us: with_halo(): after = lax.ppermute(fields[:, :HALO], 'row', down)]
    all_to_all x0 -> x12, blocking collectives: none -> 111 us  [everywhere(): over_col = lax.all_to_all(bound, 'col', 0, 0, tiled=True)]
    all_to_all x0 -> x12, starting transfers between devices: none -> 104 us  [everywhere(): lax.all_to_all(jnp.broadcast_to(merged, (row_peers, 128)), 'row', 0, 0, t...]
  transfers between devices with their start and end apart: 48 -> 16, of which waited for: 12 -> 15; matrix products, arithmetic and copies ran while one was open for 0% -> 2% of each run, Pallas kernels for 0% -> 0%
where the time goes in v1:
time: 566 us; the launch traced here: 564 us
  waiting for transfers between devices  266 us (47%)
  starting transfers between devices  127 us (22%)
  blocking collectives  111 us (20%)
  local copies, waits for them, and re-layouts  30.4 us (5%)
  Pallas kernels  16.6 us (3%)
  between operations  11 us (2%)
    all_to_all x12, waiting for transfers between devices, everywhere(): lax.all_to_all(jnp.broadcast_to(merged, (row_peers, 128)), 'row', 0, 0, t...  260 us
    all_to_all x12, blocking collectives, everywhere(): over_col = lax.all_to_all(bound, 'col', 0, 0, tiled=True)  111 us
    all_to_all x12, starting transfers between devices, everywhere(): lax.all_to_all(jnp.broadcast_to(merged, (row_peers, 128)), 'row', 0, 0, t...  104 us
    pallas_call x12, Pallas kernels, one_round(): return step(everywhere(bound), state, fixed)  16.6 us
    ppermute x1, starting transfers between devices, with_halo(): after = lax.ppermute(fields[:, :HALO], 'row', down)  16 us
    while x36, local copies, waits for them, and re-layouts  15.8 us
  transfers between devices with their start and end apart: 16, of which 15 were waited for; matrix products, arithmetic and copies ran while one was open for 2% of the time, Pallas kernels for 0%

profile of v1, /device:TPU:1, one launch (start us, length us, event | category | flops | bytes accessed | tf_op | source)
XLA Modules:
  0.0 563.8 jit_solution(16317998099625910033)
XLA Ops:
  0.6 1.6 fusion.3
  12.6 0.7 copy-done.2
  13.3 0.8 copy-done.3
  14.1 0.8 copy-done.4
  14.8 0.8 copy-done.5
  15.6 0.7 copy-done.6
  16.3 16.0 %collective-permute-start = (f32[6,12,128]{2,1,0:T(8,128)S(1)}, f32[6,12,128]{2,1,0:T(8,128)S(1)}, u32[]{:S(2)}, u32[]{:S(2)}) collective-permute-start(f32[6,12,128]{2,1,0:T(8,128)S(1)} %get-tuple-element.43), channel_id=1, source_target_pairs={{16,0},{32,16},{48,32},{64,48},{80,64},{96,80},{112,96},{128,112},... | collective-permute-start | bytes 110600 | tf_op jit(solution)/shard_map/ppermute | solution.py:30
  32.4 1.9 collective-permute-start.1
  34.3 1.2 collective-permute-done.1
  35.7 1.3 collective-permute-start.2
  37.0 4.0 collective-permute-start.3
  41.7 3.8 collective-permute-done.2
  45.4 0.9 collective-permute-done.3
  47.2 515.9 %while.12 = (s32[]{:T(128)}, f32[3,88,256]{2,1,0:T(8,128)S(1)}, f32[16,128]{1,0:T(8,128)S(1)}, f32[3,88,256]{2,1,0:T(8,128)S(1)}, s32[]{:T(128)}, /*index=5*/f32[]{:T(128)}) while((s32[]{:T(128)}, f32[3,88,256]{2,1,0:T(8,128)S(1)}, f32[16,128]{1,0:T(8,128)S(1)}, f32[3,88,256]{2,1,0:T(8,128)S(1)}, s32[]{:T(128)}, /*index=5*/f32[]{:T(128)}) %tuple.34), condition=%wide.region_3.4_spmd, body=%wide.region_1.3_spmd.sunk | while | flops 1922 | bytes 828549 | solution.py:122
  47.2 10.4 %all_to_all.17 = f32[16,1,128]{2,1,0:T(1,128)S(1)} all-to-all(f32[16,1,128]{2,1,0:T(1,128)S(1)} %bitcast.33), channel_id=1, replica_groups=mesh['row'=64,'col'=16] {'col'}, dimensions={0} | all-to-all | bytes 16384 | tf_op jit(solution)/shard_map/while/body/eval_jaxpr/all_to_all | solution.py:104
  58.3 25.8 %all-to-all-start.1 = ((f32[64,1,128]{2,1,0:T(1,128)}), f32[64,1,128]{2,1,0:T(1,128)S(1)}, u32[]{:S(2)}, u32[]{:S(2)}) async-start(f32[64,1,128]{2,1,0:T(1,128)} %broadcast_in_dim.69), calls=%async_computation.1 | async-start | bytes 65536 | tf_op jit(solution)/shard_map/while/body/eval_jaxpr/all_to_all | solution.py:106
  84.1 0.7 copy.27.refs_1_
  84.8 21.6 %all-to-all-done.1 = f32[64,1,128]{2,1,0:T(1,128)S(1)} async-done(((f32[64,1,128]{2,1,0:T(1,128)}), f32[64,1,128]{2,1,0:T(1,128)S(1)}, u32[]{:S(2)}, u32[]{:S(2)}) %all-to-all-start.1) | async-done | bytes 32800 | tf_op jit(solution)/shard_map/while/body/eval_jaxpr/all_to_all | solution.py:106
  107.0 1.4 flood_step.1
  108.4 9.1 %all_to_all.17 = f32[16,1,128]{2,1,0:T(1,128)S(1)} all-to-all(f32[16,1,128]{2,1,0:T(1,128)S(1)} %bitcast.33), channel_id=1, replica_groups=mesh['row'=64,'col'=16] {'col'}, dimensions={0} | all-to-all | bytes 16384 | tf_op jit(solution)/shard_map/while/body/eval_jaxpr/all_to_all | solution.py:104
  118.3 7.1 %all-to-all-start.1 = ((f32[64,1,128]{2,1,0:T(1,128)}), f32[64,1,128]{2,1,0:T(1,128)S(1)}, u32[]{:S(2)}, u32[]{:S(2)}) async-start(f32[64,1,128]{2,1,0:T(1,128)} %broadcast_in_dim.69), calls=%async_computation.1 | async-start | bytes 65536 | tf_op jit(solution)/shard_map/while/body/eval_jaxpr/all_to_all | solution.py:106
  125.3 0.7 copy.27.refs_1_
  126.0 21.7 %all-to-all-done.1 = f32[64,1,128]{2,1,0:T(1,128)S(1)} async-done(((f32[64,1,128]{2,1,0:T(1,128)}), f32[64,1,128]{2,1,0:T(1,128)S(1)}, u32[]{:S(2)}, u32[]{:S(2)}) %all-to-all-start.1) | async-done | bytes 32800 | tf_op jit(solution)/shard_map/while/body/eval_jaxpr/all_to_all | solution.py:106
  148.3 1.4 flood_step.1
  149.7 9.1 %all_to_all.17 = f32[16,1,128]{2,1,0:T(1,128)S(1)} all-to-all(f32[16,1,128]{2,1,0:T(1,128)S(1)} %bitcast.33), channel_id=1, replica_groups=mesh['row'=64,'col'=16] {'col'}, dimensions={0} | all-to-all | bytes 16384 | tf_op jit(solution)/shard_map/while/body/eval_jaxpr/all_to_all | solution.py:104
  159.6 7.1 %all-to-all-start.1 = ((f32[64,1,128]{2,1,0:T(1,128)}), f32[64,1,128]{2,1,0:T(1,128)S(1)}, u32[]{:S(2)}, u32[]{:S(2)}) async-start(f32[64,1,128]{2,1,0:T(1,128)} %broadcast_in_dim.69), calls=%async_computation.1 | async-start | bytes 65536 | tf_op jit(solution)/shard_map/while/body/eval_jaxpr/all_to_all | solution.py:106
  167.4 21.7 %all-to-all-done.1 = f32[64,1,128]{2,1,0:T(1,128)S(1)} async-done(((f32[64,1,128]{2,1,0:T(1,128)}), f32[64,1,128]{2,1,0:T(1,128)S(1)}, u32[]{:S(2)}, u32[]{:S(2)}) %all-to-all-start.1) | async-done | bytes 32800 | tf_op jit(solution)/shard_map/while/body/eval_jaxpr/all_to_all | solution.py:106
  189.7 1.4 flood_step.1
  191.1 9.1 %all_to_all.17 = f32[16,1,128]{2,1,0:T(1,128)S(1)} all-to-all(f32[16,1,128]{2,1,0:T(1,128)S(1)} %bitcast.33), channel_id=1, replica_groups=mesh['row'=64,'col'=16] {'col'}, dimensions={0} | all-to-all | bytes 16384 | tf_op jit(solution)/shard_map/while/body/eval_jaxpr/all_to_all | solution.py:104
  200.9 7.1 %all-to-all-start.1 = ((f32[64,1,128]{2,1,0:T(1,128)}), f32[64,1,128]{2,1,0:T(1,128)S(1)}, u32[]{:S(2)}, u32[]{:S(2)}) async-start(f32[64,1,128]{2,1,0:T(1,128)} %broadcast_in_dim.69), calls=%async_computation.1 | async-start | bytes 65536 | tf_op jit(solution)/shard_map/while/body/eval_jaxpr/all_to_all | solution.py:106
  208.7 21.7 %all-to-all-done.1 = f32[64,1,128]{2,1,0:T(1,128)S(1)} async-done(((f32[64,1,128]{2,1,0:T(1,128)}), f32[64,1,128]{2,1,0:T(1,128)S(1)}, u32[]{:S(2)}, u32[]{:S(2)}) %all-to-all-start.1) | async-done | bytes 32800 | tf_op jit(solution)/shard_map/while/body/eval_jaxpr/all_to_all | solution.py:106
  231.0 1.4 flood_step.1
  232.4 9.1 %all_to_all.17 = f32[16,1,128]{2,1,0:T(1,128)S(1)} all-to-all(f32[16,1,128]{2,1,0:T(1,128)S(1)} %bitcast.33), channel_id=1, replica_groups=mesh['row'=64,'col'=16] {'col'}, dimensions={0} | all-to-all | bytes 16384 | tf_op jit(solution)/shard_map/while/body/eval_jaxpr/all_to_all | solution.py:104
  242.2 7.1 %all-to-all-start.1 = ((f32[64,1,128]{2,1,0:T(1,128)}), f32[64,1,128]{2,1,0:T(1,128)S(1)}, u32[]{:S(2)}, u32[]{:S(2)}) async-start(f32[64,1,128]{2,1,0:T(1,128)} %broadcast_in_dim.69), calls=%async_computation.1 | async-start | bytes 65536 | tf_op jit(solution)/shard_map/while/body/eval_jaxpr/all_to_all | solution.py:106
  250.1 21.7 %all-to-all-done.1 = f32[64,1,128]{2,1,0:T(1,128)S(1)} async-done(((f32[64,1,128]{2,1,0:T(1,128)}), f32[64,1,128]{2,1,0:T(1,128)S(1)}, u32[]{:S(2)}, u32[]{:S(2)}) %all-to-all-start.1) | async-done | bytes 32800 | tf_op jit(solution)/shard_map/while/body/eval_jaxpr/all_to_all | solution.py:106
  272.3 1.4 flood_step.1
  273.8 9.1 %all_to_all.17 = f32[16,1,128]{2,1,0:T(1,128)S(1)} all-to-all(f32[16,1,128]{2,1,0:T(1,128)S(1)} %bitcast.33), channel_id=1, replica_groups=mesh['row'=64,'col'=16] {'col'}, dimensions={0} | all-to-all | bytes 16384 | tf_op jit(solution)/shard_map/while/body/eval_jaxpr/all_to_all | solution.py:104
  283.6 7.1 %all-to-all-start.1 = ((f32[64,1,128]{2,1,0:T(1,128)}), f32[64,1,128]{2,1,0:T(1,128)S(1)}, u32[]{:S(2)}, u32[]{:S(2)}) async-start(f32[64,1,128]{2,1,0:T(1,128)} %broadcast_in_dim.69), calls=%async_computation.1 | async-start | bytes 65536 | tf_op jit(solution)/shard_map/while/body/eval_jaxpr/all_to_all | solution.py:106
  291.4 21.7 %all-to-all-done.1 = f32[64,1,128]{2,1,0:T(1,128)S(1)} async-done(((f32[64,1,128]{2,1,0:T(1,128)}), f32[64,1,128]{2,1,0:T(1,128)S(1)}, u32[]{:S(2)}, u32[]{:S(2)}) %all-to-all-start.1) | async-done | bytes 32800 | tf_op jit(solution)/shard_map/while/body/eval_jaxpr/all_to_all | solution.py:106
  313.7 1.4 flood_step.1
  315.1 9.1 %all_to_all.17 = f32[16,1,128]{2,1,0:T(1,128)S(1)} all-to-all(f32[16,1,128]{2,1,0:T(1,128)S(1)} %bitcast.33), channel_id=1, replica_groups=mesh['row'=64,'col'=16] {'col'}, dimensions={0} | all-to-all | bytes 16384 | tf_op jit(solution)/shard_map/while/body/eval_jaxpr/all_to_all | solution.py:104
  324.9 7.1 %all-to-all-start.1 = ((f32[64,1,128]{2,1,0:T(1,128)}), f32[64,1,128]{2,1,0:T(1,128)S(1)}, u32[]{:S(2)}, u32[]{:S(2)}) async-start(f32[64,1,128]{2,1,0:T(1,128)} %broadcast_in_dim.69), calls=%async_computation.1 | async-start | bytes 65536 | tf_op jit(solution)/shard_map/while/body/eval_jaxpr/all_to_all | solution.py:106
  332.7 21.7 %all-to-all-done.1 = f32[64,1,128]{2,1,0:T(1,128)S(1)} async-done(((f32[64,1,128]{2,1,0:T(1,128)}), f32[64,1,128]{2,1,0:T(1,128)S(1)}, u32[]{:S(2)}, u32[]{:S(2)}) %all-to-all-start.1) | async-done | bytes 32800 | tf_op jit(solution)/shard_map/while/body/eval_jaxpr/all_to_all | solution.py:106
  355.0 1.4 flood_step.1
  356.4 9.1 %all_to_all.17 = f32[16,1,128]{2,1,0:T(1,128)S(1)} all-to-all(f32[16,1,128]{2,1,0:T(1,128)S(1)} %bitcast.33), channel_id=1, replica_groups=mesh['row'=64,'col'=16] {'col'}, dimensions={0} | all-to-all | bytes 16384 | tf_op jit(solution)/shard_map/while/body/eval_jaxpr/all_to_all | solution.py:104
  366.2 7.1 %all-to-all-start.1 = ((f32[64,1,128]{2,1,0:T(1,128)}), f32[64,1,128]{2,1,0:T(1,128)S(1)}, u32[]{:S(2)}, u32[]{:S(2)}) async-start(f32[64,1,128]{2,1,0:T(1,128)} %broadcast_in_dim.69), calls=%async_computation.1 | async-start | bytes 65536 | tf_op jit(solution)/shard_map/while/body/eval_jaxpr/all_to_all | solution.py:106
  374.1 21.7 %all-to-all-done.1 = f32[64,1,128]{2,1,0:T(1,128)S(1)} async-done(((f32[64,1,128]{2,1,0:T(1,128)}), f32[64,1,128]{2,1,0:T(1,128)S(1)}, u32[]{:S(2)}, u32[]{:S(2)}) %all-to-all-start.1) | async-done | bytes 32800 | tf_op jit(solution)/shard_map/while/body/eval_jaxpr/all_to_all | solution.py:106
  396.4 1.4 flood_step.1
  397.8 9.1 %all_to_all.17 = f32[16,1,128]{2,1,0:T(1,128)S(1)} all-to-all(f32[16,1,128]{2,1,0:T(1,128)S(1)} %bitcast.33), channel_id=1, replica_groups=mesh['row'=64,'col'=16] {'col'}, dimensions={0} | all-to-all | bytes 16384 | tf_op jit(solution)/shard_map/while/body/eval_jaxpr/all_to_all | solution.py:104
  407.6 7.1 %all-to-all-start.1 = ((f32[64,1,128]{2,1,0:T(1,128)}), f32[64,1,128]{2,1,0:T(1,128)S(1)}, u32[]{:S(2)}, u32[]{:S(2)}) async-start(f32[64,1,128]{2,1,0:T(1,128)} %broadcast_in_dim.69), calls=%async_computation.1 | async-start | bytes 65536 | tf_op jit(solution)/shard_map/while/body/eval_jaxpr/all_to_all | solution.py:106
  415.4 21.7 %all-to-all-done.1 = f32[64,1,128]{2,1,0:T(1,128)S(1)} async-done(((f32[64,1,128]{2,1,0:T(1,128)}), f32[64,1,128]{2,1,0:T(1,128)S(1)}, u32[]{:S(2)}, u32[]{:S(2)}) %all-to-all-start.1) | async-done | bytes 32800 | tf_op jit(solution)/shard_map/while/body/eval_jaxpr/all_to_all | solution.py:106
  437.7 1.4 flood_step.1
  439.1 9.1 %all_to_all.17 = f32[16,1,128]{2,1,0:T(1,128)S(1)} all-to-all(f32[16,1,128]{2,1,0:T(1,128)S(1)} %bitcast.33), channel_id=1, replica_groups=mesh['row'=64,'col'=16] {'col'}, dimensions={0} | all-to-all | bytes 16384 | tf_op jit(solution)/shard_map/while/body/eval_jaxpr/all_to_all | solution.py:104
  448.9 7.1 %all-to-all-start.1 = ((f32[64,1,128]{2,1,0:T(1,128)}), f32[64,1,128]{2,1,0:T(1,128)S(1)}, u32[]{:S(2)}, u32[]{:S(2)}) async-start(f32[64,1,128]{2,1,0:T(1,128)} %broadcast_in_dim.69), calls=%async_computation.1 | async-start | bytes 65536 | tf_op jit(solution)/shard_map/while/body/eval_jaxpr/all_to_all | solution.py:106
  456.8 21.7 %all-to-all-done.1 = f32[64,1,128]{2,1,0:T(1,128)S(1)} async-done(((f32[64,1,128]{2,1,0:T(1,128)}), f32[64,1,128]{2,1,0:T(1,128)S(1)}, u32[]{:S(2)}, u32[]{:S(2)}) %all-to-all-start.1) | async-done | bytes 32800 | tf_op jit(solution)/shard_map/while/body/eval_jaxpr/all_to_all | solution.py:106
  479.0 1.4 flood_step.1
  480.4 9.1 %all_to_all.17 = f32[16,1,128]{2,1,0:T(1,128)S(1)} all-to-all(f32[16,1,128]{2,1,0:T(1,128)S(1)} %bitcast.33), channel_id=1, replica_groups=mesh['row'=64,'col'=16] {'col'}, dimensions={0} | all-to-all | bytes 16384 | tf_op jit(solution)/shard_map/while/body/eval_jaxpr/all_to_all | solution.py:104
  490.3 7.1 %all-to-all-start.1 = ((f32[64,1,128]{2,1,0:T(1,128)}), f32[64,1,128]{2,1,0:T(1,128)S(1)}, u32[]{:S(2)}, u32[]{:S(2)}) async-start(f32[64,1,128]{2,1,0:T(1,128)} %broadcast_in_dim.69), calls=%async_computation.1 | async-start | bytes 65536 | tf_op jit(solution)/shard_map/while/body/eval_jaxpr/all_to_all | solution.py:106
  498.1 21.7 %all-to-all-done.1 = f32[64,1,128]{2,1,0:T(1,128)S(1)} async-done(((f32[64,1,128]{2,1,0:T(1,128)}), f32[64,1,128]{2,1,0:T(1,128)S(1)}, u32[]{:S(2)}, u32[]{:S(2)}) %all-to-all-start.1) | async-done | bytes 32800 | tf_op jit(solution)/shard_map/while/body/eval_jaxpr/all_to_all | solution.py:106
  520.4 1.4 flood_step.1
  521.8 9.1 %all_to_all.17 = f32[16,1,128]{2,1,0:T(1,128)S(1)} all-to-all(f32[16,1,128]{2,1,0:T(1,128)S(1)} %bitcast.33), channel_id=1, replica_groups=mesh['row'=64,'col'=16] {'col'}, dimensions={0} | all-to-all | bytes 16384 | tf_op jit(solution)/shard_map/while/body/eval_jaxpr/all_to_all | solution.py:104
  531.6 7.1 %all-to-all-start.1 = ((f32[64,1,128]{2,1,0:T(1,128)}), f32[64,1,128]{2,1,0:T(1,128)S(1)}, u32[]{:S(2)}, u32[]{:S(2)}) async-start(f32[64,1,128]{2,1,0:T(1,128)} %broadcast_in_dim.69), calls=%async_computation.1 | async-start | bytes 65536 | tf_op jit(solution)/shard_map/while/body/eval_jaxpr/all_to_all | solution.py:106
  539.4 21.7 %all-to-all-done.1 = f32[64,1,128]{2,1,0:T(1,128)S(1)} async-done(((f32[64,1,128]{2,1,0:T(1,128)}), f32[64,1,128]{2,1,0:T(1,128)S(1)}, u32[]{:S(2)}, u32[]{:S(2)}) %all-to-all-start.1) | async-done | bytes 32800 | tf_op jit(solution)/shard_map/while/body/eval_jaxpr/all_to_all | solution.py:106
  561.7 1.4 flood_step.1
  (82 shorter events, 24.9 us)
Async XLA Ops:
  0.6 11.9 %copy-start.1 = (f32[64,128]{1,0:T(8,128)S(1)}, f32[64,128]{1,0:T(8,128)}, u32[]{:S(2)}) copy-start(f32[64,128]{1,0:T(8,128)} %param.9) | copy-start | bytes 98308
  12.5 0.8 copy-start.2
  13.3 0.8 copy-start.3
  14.0 0.8 copy-start.4
  14.8 0.8 copy-start.5
  15.6 0.8 copy-start.6
  16.3 18.0 %collective-permute-start = (f32[6,12,128]{2,1,0:T(8,128)S(1)}, f32[6,12,128]{2,1,0:T(8,128)S(1)}, u32[]{:S(2)}, u32[]{:S(2)}) collective-permute-start(f32[6,12,128]{2,1,0:T(8,128)S(1)} %get-tuple-element.43), channel_id=1, source_target_pairs={{16,0},{32,16},{48,32},{64,48},{80,64},{96,80},{112,96},{128,112},... | collective-permute-start | bytes 110600 | tf_op jit(solution)/shard_map/ppermute | solution.py:30
  32.4 3.1 collective-permute-start.1
  35.7 9.8 %collective-permute-start.2 = (f32[6,88,12]{2,1,0:T(8,128)S(1)}, f32[6,88,12]{2,1,0:T(8,128)S(1)}, u32[]{:S(2)}, u32[]{:S(2)}) collective-permute-start(f32[6,88,12]{2,1,0:T(8,128)S(1)} %get-tuple-element.41), channel_id=1, source_target_pairs={{1,0},{2,1},{3,2},{4,3},{5,4},{6,5},{7,6},{8,7},{9,8},{10,9},{11,1... | collective-permute-start | bytes 76040 | tf_op jit(solution)/shard_map/ppermute | solution.py:34
  37.0 9.4 %collective-permute-start.3 = (f32[6,88,12]{2,1,0:T(8,128)S(1)}, f32[6,88,12]{2,1,0:T(8,128)S(1)}, u32[]{:S(2)}, u32[]{:S(2)}) collective-permute-start(f32[6,88,12]{2,1,0:T(8,128)S(1)} %get-tuple-element.42), channel_id=1, source_target_pairs={{0,1},{1,2},{2,3},{3,4},{4,5},{5,6},{6,7},{7,8},{8,9},{9,10},{10,1... | collective-permute-start | bytes 76040 | tf_op jit(solution)/shard_map/ppermute | solution.py:33
  58.3 48.1 %all-to-all-start.1 = ((f32[64,1,128]{2,1,0:T(1,128)}), f32[64,1,128]{2,1,0:T(1,128)S(1)}, u32[]{:S(2)}, u32[]{:S(2)}) async-start(f32[64,1,128]{2,1,0:T(1,128)} %broadcast_in_dim.69), calls=%async_computation.1 | async-start | bytes 65536 | tf_op jit(solution)/shard_map/while/body/eval_jaxpr/all_to_all | solution.py:106
  106.4 0.6 copy-start
  118.3 29.5 %all-to-all-start.1 = ((f32[64,1,128]{2,1,0:T(1,128)}), f32[64,1,128]{2,1,0:T(1,128)S(1)}, u32[]{:S(2)}, u32[]{:S(2)}) async-start(f32[64,1,128]{2,1,0:T(1,128)} %broadcast_in_dim.69), calls=%async_computation.1 | async-start | bytes 65536 | tf_op jit(solution)/shard_map/while/body/eval_jaxpr/all_to_all | solution.py:106
  147.7 0.6 copy-start
  159.6 29.5 %all-to-all-start.1 = ((f32[64,1,128]{2,1,0:T(1,128)}), f32[64,1,128]{2,1,0:T(1,128)S(1)}, u32[]{:S(2)}, u32[]{:S(2)}) async-start(f32[64,1,128]{2,1,0:T(1,128)} %broadcast_in_dim.69), calls=%async_computation.1 | async-start | bytes 65536 | tf_op jit(solution)/shard_map/while/body/eval_jaxpr/all_to_all | solution.py:106
  189.1 0.6 copy-start
  200.9 29.5 %all-to-all-start.1 = ((f32[64,1,128]{2,1,0:T(1,128)}), f32[64,1,128]{2,1,0:T(1,128)S(1)}, u32[]{:S(2)}, u32[]{:S(2)}) async-start(f32[64,1,128]{2,1,0:T(1,128)} %broadcast_in_dim.69), calls=%async_computation.1 | async-start | bytes 65536 | tf_op jit(solution)/shard_map/while/body/eval_jaxpr/all_to_all | solution.py:106
  230.4 0.6 copy-start
  242.2 29.5 %all-to-all-start.1 = ((f32[64,1,128]{2,1,0:T(1,128)}), f32[64,1,128]{2,1,0:T(1,128)S(1)}, u32[]{:S(2)}, u32[]{:S(2)}) async-start(f32[64,1,128]{2,1,0:T(1,128)} %broadcast_in_dim.69), calls=%async_computation.1 | async-start | bytes 65536 | tf_op jit(solution)/shard_map/while/body/eval_jaxpr/all_to_all | solution.py:106
  271.7 0.6 copy-start
  283.6 29.5 %all-to-all-start.1 = ((f32[64,1,128]{2,1,0:T(1,128)}), f32[64,1,128]{2,1,0:T(1,128)S(1)}, u32[]{:S(2)}, u32[]{:S(2)}) async-start(f32[64,1,128]{2,1,0:T(1,128)} %broadcast_in_dim.69), calls=%async_computation.1 | async-start | bytes 65536 | tf_op jit(solution)/shard_map/while/body/eval_jaxpr/all_to_all | solution.py:106
  313.1 0.6 copy-start
  324.9 29.5 %all-to-all-start.1 = ((f32[64,1,128]{2,1,0:T(1,128)}), f32[64,1,128]{2,1,0:T(1,128)S(1)}, u32[]{:S(2)}, u32[]{:S(2)}) async-start(f32[64,1,128]{2,1,0:T(1,128)} %broadcast_in_dim.69), calls=%async_computation.1 | async-start | bytes 65536 | tf_op jit(solution)/shard_map/while/body/eval_jaxpr/all_to_all | solution.py:106
  354.4 0.6 copy-start
  366.2 29.5 %all-to-all-start.1 = ((f32[64,1,128]{2,1,0:T(1,128)}), f32[64,1,128]{2,1,0:T(1,128)S(1)}, u32[]{:S(2)}, u32[]{:S(2)}) async-start(f32[64,1,128]{2,1,0:T(1,128)} %broadcast_in_dim.69), calls=%async_computation.1 | async-start | bytes 65536 | tf_op jit(solution)/shard_map/while/body/eval_jaxpr/all_to_all | solution.py:106
  395.8 0.6 copy-start
  407.6 29.5 %all-to-all-start.1 = ((f32[64,1,128]{2,1,0:T(1,128)}), f32[64,1,128]{2,1,0:T(1,128)S(1)}, u32[]{:S(2)}, u32[]{:S(2)}) async-start(f32[64,1,128]{2,1,0:T(1,128)} %broadcast_in_dim.69), calls=%async_computation.1 | async-start | bytes 65536 | tf_op jit(solution)/shard_map/while/body/eval_jaxpr/all_to_all | solution.py:106
  437.1 0.6 copy-start
  448.9 29.5 %all-to-all-start.1 = ((f32[64,1,128]{2,1,0:T(1,128)}), f32[64,1,128]{2,1,0:T(1,128)S(1)}, u32[]{:S(2)}, u32[]{:S(2)}) async-start(f32[64,1,128]{2,1,0:T(1,128)} %broadcast_in_dim.69), calls=%async_computation.1 | async-start | bytes 65536 | tf_op jit(solution)/shard_map/while/body/eval_jaxpr/all_to_all | solution.py:106
  478.4 0.6 copy-start
  490.3 29.5 %all-to-all-start.1 = ((f32[64,1,128]{2,1,0:T(1,128)}), f32[64,1,128]{2,1,0:T(1,128)S(1)}, u32[]{:S(2)}, u32[]{:S(2)}) async-start(f32[64,1,128]{2,1,0:T(1,128)} %broadcast_in_dim.69), calls=%async_computation.1 | async-start | bytes 65536 | tf_op jit(solution)/shard_map/while/body/eval_jaxpr/all_to_all | solution.py:106
  519.8 0.6 copy-start
  531.6 29.5 %all-to-all-start.1 = ((f32[64,1,128]{2,1,0:T(1,128)}), f32[64,1,128]{2,1,0:T(1,128)S(1)}, u32[]{:S(2)}, u32[]{:S(2)}) async-start(f32[64,1,128]{2,1,0:T(1,128)} %broadcast_in_dim.69), calls=%async_computation.1 | async-start | bytes 65536 | tf_op jit(solution)/shard_map/while/body/eval_jaxpr/all_to_all | solution.py:106
  561.1 0.6 copy-start
